TPU v7x, 1024 devices: a whole 4x8x16 slice. The times are simulated.
1024 devices in a mesh: dp: 8 (over y), ctx: 32 (over z, core), tensor: 4 (over x).
Axes of the slice: x: 4, y: 8, z: 16, core: 2. Of those that a mesh axis runs over, the one named last changes fastest.
Arguments:
- mamba_input: bfloat16 [32768, 4096], P(('dp', 'ctx'), 'tensor'), parts along dimension 0, may hold values from -140 to 140
- mamba_gate: bfloat16 [32768, 4096], P(('dp', 'ctx'), 'tensor'), parts along dimension 0, may hold values from -6 to 6
- state_write: bfloat16 [32768, 512], P(('dp', 'ctx'), 'tensor'), parts along dimension 0, may hold values from -1.796875 to 1.796875
- state_read: bfloat16 [32768, 512], P(('dp', 'ctx'), 'tensor'), parts along dimension 0, may hold values from -1.796875 to 1.796875
- step_size: float32 [32768, 64], P(('dp', 'ctx'), 'tensor'), parts along dimension 0, may hold values from 0.25 to 4
- decay_rate: float32 [64], P('tensor'), may hold values from 4.8828125e-05 to 0.034
- skip_scale: float32 [64], P('tensor'), may hold values from 1 to 8
- norm_gain: float32 [4096], P('tensor'), may hold values from 0.5 to 1.5
- query_rows: bfloat16 [32768, 2048], P(('dp', 'ctx'), 'tensor'), parts along dimension 0, may hold values from -10 to 10
- key_rows: bfloat16 [32768, 512], P(('dp', 'ctx'), 'tensor'), parts along dimension 0, may hold values from -10 to 10
- value_rows: bfloat16 [32768, 512], P(('dp', 'ctx'), 'tensor'), parts along dimension 0, may hold values from -6 to 6
- doc_offsets: int32 [264], P('dp'), parts along dimension 0, may hold values from 0 to 4096, as said below
Outputs:
- mamba_out: bfloat16 [32768, 4096], P(('dp', 'ctx'), 'tensor'), parts along dimension 0
- attn_out: bfloat16 [32768, 2048], P(('dp', 'ctx'), 'tensor'), parts along dimension 0
There are 8 independent parts, one for each index of `dp`. A program takes and returns all parts, laid end to end along the dimension named above; an argument that names none is the same for every part. Nothing has to cross between parts.
Inputs may be any that keep to these rules, and one draw needn't show every extreme that they name: doc_offsets[0] is 0 and doc_offsets[32] is 4096; the offsets rise strictly; every document holds 1 to 3072 tokens and one holds exactly 3072.
All inputs are finite; a program needn't handle non-finite values.
Results may differ from a plain program's by a relative error of at most 0.0085.
Values may be sent and summed in bfloat16 or wider, within the bound.
A program may use at most 64 MiB of HBM per device.

v0:
```python
import math

import jax
import jax.numpy as jnp
from jax import lax
from jax.sharding import PartitionSpec as P

MP = 64
MN = 128
HD = 128


def entering(value, axis, combine, identity):
    size, position = (lax.axis_size(axis), lax.axis_index(axis))
    everything = jax.tree.map(lambda part: lax.all_gather(part, axis), value)
    start = jax.tree.map(
        lambda part, zero: jnp.broadcast_to(jnp.asarray(zero, part.dtype), part.shape),
        value,
        identity,
    )

    def step(k, before):
        reached = k < position
        new = combine(before, jax.tree.map(lambda part: part[k], everything))
        return jax.tree.map(lambda a, b: jnp.where(reached, a, b), new, before)

    return lax.fori_loop(0, size, step, start)


def doc_index(positions, doc_offsets):
    interior = doc_offsets[1:-1]
    return jnp.sum((positions[:, None] >= interior[None, :]).astype(jnp.int32), axis=1)


def doc_first(positions, doc_offsets):
    return jnp.any(positions[:, None] == doc_offsets[None, :-1], axis=1)


def chain_combine(earlier, later):
    return (earlier[0] * later[0], later[0][:, None, None] * earlier[1] + later[1])


def per_device(
    mamba_input,
    mamba_gate,
    state_write,
    state_read,
    step_size,
    decay_rate,
    skip_scale,
    norm_gain,
    query_rows,
    key_rows,
    value_rows,
    doc_offsets,
):
    highest = lax.Precision.HIGHEST
    count = mamba_input.shape[0]
    head_count = step_size.shape[1]
    group_count = state_write.shape[1] // MN
    per_group = head_count // group_count
    anchor = lax.axis_index("ctx") * count
    positions = anchor + jnp.arange(count, dtype=jnp.int32)
    segment = jnp.cumsum(doc_first(positions, doc_offsets).astype(jnp.int32))
    running = jnp.cumsum(-decay_rate[None, :] * step_size, axis=0)
    inputs = mamba_input.reshape(count, head_count, MP).astype(jnp.float32)
    scaled = inputs * step_size[:, :, None]
    writes = state_write.reshape(count, group_count, MN)
    reads = state_read.reshape(count, group_count, MN)
    intersection = jnp.einsum("tgn,sgn->gts", reads, writes, preferred_element_type=jnp.float32)
    order_ids = jnp.arange(count, dtype=jnp.int32)
    same = (segment[:, None] == segment[None, :]) & (order_ids[:, None] >= order_ids[None, :])
    trail = running.T
    spread = jnp.where(same[None], trail[:, :, None] - trail[:, None, :], jnp.float32(0.0))
    kernel = jnp.where(same[None], jnp.exp(spread), jnp.float32(0.0)).reshape(
        group_count, per_group, count, count
    )
    weight = (kernel * intersection[:, None]).reshape(head_count, count, count)
    inside = jnp.einsum("hts,shp->thp", weight, scaled, precision=highest)
    ending = jnp.where(
        (segment == segment[-1])[:, None], jnp.exp(running[-1][None, :] - running), jnp.float32(0.0)
    )
    ended = (scaled * ending[:, :, None]).reshape(count, group_count, per_group, MP)
    summary = jnp.einsum(
        "tgn,tgqp->gqnp", writes.astype(jnp.float32), ended, precision=highest
    ).reshape(head_count, MN, MP)
    through = jnp.where(segment[-1] == 0, jnp.exp(running[-1]), jnp.float32(0.0))
    carried_in = entering(
        (through, summary), "ctx", chain_combine, (jnp.ones_like(through), jnp.zeros_like(summary))
    )
    incoming = carried_in[1].reshape(group_count, per_group, MN, MP)
    entry = jnp.where((segment == 0)[:, None], jnp.exp(running), jnp.float32(0.0))
    carried = (
        jnp.einsum(
            "tgn,gqnp->tgqp", reads.astype(jnp.float32), incoming, precision=highest
        ).reshape(count, head_count, MP)
        * entry[:, :, None]
    )
    mixed = inside + carried + skip_scale[None, :, None] * inputs
    gated = mixed * jax.nn.silu(mamba_gate.reshape(count, head_count, MP).astype(jnp.float32))
    grouped = gated.reshape(count, group_count, per_group * MP)
    normed = grouped * lax.rsqrt(jnp.mean(grouped * grouped, axis=-1, keepdims=True) + 1e-05)
    mamba_out = (normed.reshape(count, head_count * MP) * norm_gain[None, :]).astype(jnp.bfloat16)
    kv_local = key_rows.shape[1] // HD
    query_local = query_rows.shape[1] // HD
    per_kv = query_local // kv_local
    query_doc = doc_index(positions, doc_offsets)
    queries = query_rows.reshape(count, kv_local, per_kv, HD)
    top = jnp.full((kv_local, per_kv, count), -1e30, jnp.float32)
    piece_keys = lax.all_gather(key_rows, "ctx", axis=0, tiled=True)
    piece_values = lax.all_gather(value_rows, "ctx", axis=0, tiled=True)
    span = piece_keys.shape[0]
    key_pos = jnp.arange(span, dtype=jnp.int32)
    key_doc = doc_index(key_pos, doc_offsets)
    visible = (key_doc[None, :] == query_doc[:, None]) & (key_pos[None, :] <= positions[:, None])
    scores = jnp.einsum(
        "tgqd,sgd->gqts",
        queries,
        piece_keys.reshape(span, kv_local, HD),
        preferred_element_type=jnp.float32,
    ) / math.sqrt(HD)
    scores = jnp.where(visible[None, None], scores, jnp.float32(-1e30))
    fresh = jnp.maximum(top, jnp.max(scores, axis=-1))
    expo = jnp.where(visible[None, None], jnp.exp(scores - fresh[:, :, :, None]), jnp.float32(0.0))
    total = jnp.sum(expo, axis=-1)
    update = jnp.einsum(
        "gqts,sgd->gqtd",
        expo.astype(jnp.bfloat16),
        piece_values.reshape(span, kv_local, HD),
        preferred_element_type=jnp.float32,
    )
    result = update / total[:, :, :, None]
    attn_out = result.transpose(2, 0, 1, 3).reshape(count, query_local * HD).astype(jnp.bfloat16)
    return (mamba_out, attn_out)


def solution(mesh):
    in_specs = (
        P(("dp", "ctx"), "tensor"),
        P(("dp", "ctx"), "tensor"),
        P(("dp", "ctx"), "tensor"),
        P(("dp", "ctx"), "tensor"),
        P(("dp", "ctx"), "tensor"),
        P("tensor"),
        P("tensor"),
        P("tensor"),
        P(("dp", "ctx"), "tensor"),
        P(("dp", "ctx"), "tensor"),
        P(("dp", "ctx"), "tensor"),
        P("dp"),
    )
    out_specs = (P(("dp", "ctx"), "tensor"), P(("dp", "ctx"), "tensor"))
    return jax.shard_map(
        per_device, mesh=mesh, in_specs=in_specs, out_specs=out_specs, check_vma=False
    )
```

profile of v0, /device:TPU:1, one launch (start us, length us, event | category | flops | bytes accessed | tf_op | source)
XLA Modules:
  0.0 365.8 jit_solution(8154760879744056008)
XLA Ops:
  8.0 1.5 copy.72
  14.4 1.1 copy.60
  16.3 1.9 convolution_bitcast_fusion
  20.8 45.3 %all-gather = f32[32,1,16]{2,1,0:T(1,128)} all-gather(f32[1,1,16]{2,1,0:T(1,128)S(1)} %get-tuple-element.156), channel_id=1, replica_groups=mesh['dp'=8,'ctx'=32,'tensor'=4] {'ctx'}, dimensions={0}, use_global_device_ids=true | all-gather | bytes 2112 | tf_op jit(solution)/shard_map/all_gather | solution.py:15
  67.0 1.6 fusion.45
  68.5 1.8 fusion.8
  70.4 23.8 %all-gather.7.cloned.1.call-done = bf16[4096,128]{1,0:T(8,128)(2,1)} async-done(((bf16[128,128]{1,0:T(8,128)(2,1)}), bf16[4096,128]{1,0:T(8,128)(2,1)}) %all-gather.7.cloned.1.call-update) | async-done | bytes 1048592 | tf_op jit(solution)/shard_map/all_gather | solution.py:110
  94.1 2.5 fusion.1
  96.7 3.2 copy-done.1
  99.9 2.1 fusion.2
  101.9 65.6 %all-gather.9.cloned.1.call-done = bf16[4096,128]{0,1:T(8,128)(2,1)} async-done(((bf16[128,128]{0,1:T(8,128)(2,1)}), bf16[4096,128]{0,1:T(8,128)(2,1)}) %all-gather.9.cloned.1.call-update) | async-done | bytes 1048592 | tf_op jit(solution)/shard_map/all_gather | solution.py:111
  167.5 5.6 %fusion.16 = bf16[4,128,128]{1,2,0:T(8,128)(2,1)S(1)} fusion(f32[4096,128,4]{1,0,2:T(8,128)} %copy-done.1, f32[4,128]{1,0:T(4,128)S(1)} %broadcast_maximum_fusion, pred[128,4096]{0,1:T(8,128)(4,1)S(1)} %fusion.8, bf16[4096,128]{0,1:T(8,128)(2,1)} %all-gather.9.cloned.1.call-done, f32[4,128]{1,0:T(4,128)S(1)} %fusion.2), kind=kOutput, calls=%fused_computation.22 | convolution fusion | flops 547487744 | bytes 10096640 | tf_op jit(solution)/shard_map/gqts,sgd->gqtd/dot_general | solution.py:126
  173.9 102.8 %all-gather.5.cloned.1.call-done = f32[32,16,128,64]{2,3,1,0:T(8,128)} async-done(((f32[1,16,128,64]{2,3,1,0:T(8,128)}), f32[32,16,128,64]{2,3,1,0:T(8,128)}) %all-gather.5.cloned.1.call-update) | async-done | bytes 16777232 | tf_op jit(solution)/shard_map/all_gather | solution.py:15
  276.7 76.1 %while.14 = (s32[]{:T(128)}, f32[16,128,64]{2,1,0:T(8,128)S(1)}, s32[]{:T(128)}, f32[32,16]{1,0:T(8,128)}, f32[32,16,128,64]{2,3,1,0:T(8,128)}, /*index=5*/s32[]{:T(128)}, s32[]{:T(128)}) while((s32[]{:T(128)}, f32[16,128,64]{2,1,0:T(8,128)S(1)}, s32[]{:T(128)}, f32[32,16]{1,0:T(8,128)}, f32[32,16,128,64]{2,3,1,0:T(8,128)}, ...), condition=%wide.region_4.5_spmd.clone, body=%wide.region_3.4_spmd.clone.sunk | while | flops 524292 | bytes 3670313 | solution.py:27
  276.7 1.1 constant_dynamic-slice_fusion.2
  283.8 1.1 constant_dynamic-slice_fusion.2
  288.6 1.1 constant_dynamic-slice_fusion.2
  295.7 1.1 constant_dynamic-slice_fusion.2
  307.6 1.1 constant_dynamic-slice_fusion.2
  310.0 1.1 constant_dynamic-slice_fusion.2
  319.5 1.1 constant_dynamic-slice_fusion.2
  352.8 1.7 fusion.11
  354.6 3.0 multiply_reduce_fusion
  357.8 1.5 multiply_convert_fusion
  (160 shorter events, 77.8 us)
Async XLA Ops:
  7.2 87.0 %copy-start = (bf16[128,512]{1,0:T(8,128)(2,1)S(1)}, bf16[128,512]{1,0:T(8,128)(2,1)}, u32[]{:S(2)}) copy-start(bf16[128,512]{1,0:T(8,128)(2,1)} %param.22) | copy-start | bytes 393220
  7.2 87.0 %all-gather.7.cloned.1.call-start = ((), (), s32[]{:S(2)}) async-start(), calls=%async_computation.1 | async-start | bytes 1081344 | tf_op jit(solution)/shard_map/all_gather | solution.py:110
  7.9 159.6 %all-gather.9.cloned.1.call-start = ((), (), s32[]{:S(2)}) async-start(), calls=%async_computation.2 | async-start | bytes 1081344 | tf_op jit(solution)/shard_map/all_gather | solution.py:111
  9.5 267.2 %all-gather.5.cloned.1.call-start = ((), (), s32[]{:S(2)}) async-start(), calls=%async_computation | async-start | bytes 17301504 | tf_op jit(solution)/shard_map/all_gather | solution.py:15
  96.6 3.2 copy-start.1
  276.7 77.9 %copy-start.2 = (f32[128,16]{0,1:T(8,128)S(1)}, f32[128,16]{0,1:T(8,128)}, u32[]{:S(2)}) copy-start(f32[128,16]{0,1:T(8,128)} %param.18) | copy-start | bytes 24580
Sparse Core Ops, SparseCore 0:
  10.7 83.4 all-gather.6
  97.3 70.1 all-gather.8
  170.2 106.4 all-gather.4
where the time goes:
time: 369 us; the launch traced here: 366 us
  waiting for transfers between devices  193 us (52%)
  local copies, waits for them, and re-layouts  77.5 us (21%)
  blocking collectives  45.3 us (12%)
  other arithmetic  18.3 us (5%)
  matrix products  16.3 us (4%)
  between operations  14.6 us (4%)
    all_gather x1, waiting for transfers between devices, entering(): everything = jax.tree.map(lambda part: lax.all_gather(part, axis), value)  103 us
    all_gather x1, waiting for transfers between devices, per_device(): piece_values = lax.all_gather(value_rows, 'ctx', axis=0, tiled=True)  65.6 us
    dynamic_slice x64, local copies, waits for them, and re-layouts, step(): new = combine(before, jax.tree.map(lambda part: part[k], everything))  45.3 us
    all_gather x1, blocking collectives, entering(): everything = jax.tree.map(lambda part: lax.all_gather(part, axis), value)  45.3 us
    all_gather x1, waiting for transfers between devices, per_device(): piece_keys = lax.all_gather(key_rows, 'ctx', axis=0, tiled=True)  23.8 us
    mul x32, local copies, waits for them, and re-layouts, chain_combine(): later[0][:, None, None] * earlier[1] + later[1]  22.1 us
    select_n x32, other arithmetic, step(): return jax.tree.map(lambda a, b: jnp.where(reached, a, b), new, before)  7.75 us
  transfers between devices with their start and end apart: 3, of which 3 were waited for; matrix products, arithmetic and copies ran while one was open for 7% of the time, Pallas kernels for 0%

commit v1 on v0

v1 whole, which is shorter than its diff:
```python
import functools
import math

import jax
import jax.numpy as jnp
from jax import lax
from jax.experimental import pallas as pl
from jax.experimental.pallas import tpu as pltpu
from jax.sharding import PartitionSpec as P

MESH = pl.DeviceIdType.MESH
HIGHEST = lax.Precision.HIGHEST
F32, BF16 = jnp.float32, jnp.bfloat16

MP = 64
HD = 128
TOK = 128
CHIPS = 16
HEADS = 16
COLS = HEADS * MP
TILES = COLS // 128
NEAR = 7
FAR = 12
NEG = -1e30
SCALE = math.log2(math.e) / math.sqrt(HD)


def nt_dot(a, b):
    return lax.dot_general(a, b, (((1,), (1,)), ((), ())), preferred_element_type=F32)


def tn_dot(a, b):
    return lax.dot_general(a, b, (((0,), (0,)), ((), ())), preferred_element_type=F32)


def spread(table, tile):
    rows = table.shape[0]
    lane = lax.broadcasted_iota(jnp.int32, (rows, 128), 1)
    return jnp.where(lane < MP, table[:, 2 * tile : 2 * tile + 1], table[:, 2 * tile + 1 : 2 * tile + 2])


def kernel(
    offs_ref,
    step_ref,
    rate_ref,
    skip_ref,
    gain_ref,
    x_hbm,
    gate_hbm,
    write_hbm,
    read_hbm,
    q_hbm,
    k_hbm,
    v_hbm,
    mamba_ref,
    attn_ref,
    x_ref,
    gate_ref,
    b_ref,
    c_ref,
    q_ref,
    kv_ref,
    u_ref,
    lhs_ref,
    er_ref,
    own_ref,
    own_send,
    part_ref,
    thr_own,
    thr_part,
    comb_ref,
    comb_thr,
    in1_ref,
    thr1_ref,
    pre_ref,
    in2_ref,
    state_ref,
    other_ref,
    start_ref,
    qpos_ref,
    top_ref,
    acc_ref,
    gated_ref,
    load_sem,
    near_recv,
    pair_recv,
    near_send,
    pair_send,
    ex_send,
    ex_recv,
    s1_send,
    s1_recv,
    t1_send,
    t1_recv,
    s2_send,
    s2_recv,
):
    me = lax.axis_index("ctx")
    z, core = lax.div(me, 2), lax.rem(me, 2)
    partner = me + 1 - 2 * core
    anchor = me * TOK

    def chip(index):
        return {"ctx": 2 * index + core}

    def remote(src, dst, send, recv, device):
        return pltpu.make_async_remote_copy(
            src_ref=src, dst_ref=dst, send_sem=send, recv_sem=recv, device_id=device, device_id_type=MESH
        )

    def peer(k):
        turn = lax.div(k + 1, 2)
        away = CHIPS // 2 + jnp.where(lax.rem(k, 2) == 1, turn, -turn)
        return lax.rem(z + away, CHIPS)

    barrier = pltpu.get_barrier_semaphore()

    def greet(k, _):
        pl.semaphore_signal(barrier, inc=1, device_id=chip(peer(k)), device_id_type=MESH)
        return 0

    lax.fori_loop(0, CHIPS - 1, greet, 0)
    pl.semaphore_signal(barrier, inc=1, device_id={"ctx": partner}, device_id_type=MESH)

    loads = [
        pltpu.make_async_copy(src, dst, load_sem.at[n])
        for n, (src, dst) in enumerate(
            (
                (k_hbm, kv_ref.at[0, core, 0]),
                (v_hbm, kv_ref.at[0, core, 1]),
                (write_hbm, b_ref),
                (read_hbm, c_ref),
                (x_hbm, x_ref),
                (q_hbm, q_ref),
                (gate_hbm, gate_ref),
            )
        )
    ]
    for load in loads:
        load.start()

    row = lax.broadcasted_iota(jnp.int32, (TOK, 128), 0)
    col = lax.broadcasted_iota(jnp.int32, (TOK, 128), 1)
    pos = anchor + row
    start = jnp.zeros((TOK, 128), jnp.int32)
    final = jnp.zeros((8, 128), jnp.int32)
    for d in range(1, 32):
        off = offs_ref[d]
        start = jnp.where(pos >= off, off, start)
        final = jnp.where(anchor + TOK - 1 + jnp.zeros((8, 128), jnp.int32) >= off, off, final)
    final = final[0:1]
    start_ref[...] = start
    qpos_ref[...] = pos

    lower = (col <= row).astype(F32)
    running = jnp.dot(lower, -rate_ref[...] * step_ref[...], precision=HIGHEST, preferred_element_type=F32)
    grow = jnp.exp(-running) * step_ref[...]
    er_ref[...] = jnp.exp(running)
    last = jnp.exp(running[TOK - 1 : TOK])

    for load in loads[:5]:
        load.wait()
    held = jnp.where(pos >= final, b_ref[...].astype(F32), 0.0)
    held_t = held.T.astype(BF16)
    inner = jnp.where((col <= row) & (anchor + col >= start), nt_dot(c_ref[...], b_ref[...]), 0.0)
    entering = jnp.where(start < anchor, c_ref[...].astype(F32), 0.0)
    lhs_ref[:, 0:128] = inner.astype(BF16)
    lhs_ref[:, 128:256] = entering.astype(BF16)
    for t in range(TILES):
        sl = slice(128 * t, 128 * t + 128)
        u = (x_ref[:, sl].astype(F32) * spread(grow, t)).astype(BF16)
        u_ref[:, sl] = u
        decay = spread(last, t)
        tile = jnp.dot(held_t, u, preferred_element_type=F32) * decay
        own_ref[4 * t : 4 * t + 4] = tile.reshape(4, 32, 128)
        own_send[4 * t : 4 * t + 4] = tile.astype(BF16).reshape(4, 32, 128)
        thr_own[t] = jnp.where(final < anchor, decay, 0.0)

    pl.semaphore_wait(barrier, CHIPS)

    def forward(d):
        return remote(kv_ref.at[d, core], kv_ref.at[d + 1, core], near_send.at[d], near_recv.at[d + 1], chip(z + 1))

    def backward(d):
        return remote(kv_ref.at[d, core], kv_ref.at[d - 1, core], near_send.at[d], near_recv.at[d - 1], chip(z - 1))

    def direct():
        target = jnp.minimum(z + FAR, CHIPS - 1)
        return remote(
            kv_ref.at[0, core], kv_ref.at[target - z, core], near_send.at[NEAR], near_recv.at[target - z], chip(target)
        )

    def pair(d):
        return remote(kv_ref.at[d, core], kv_ref.at[d, core], pair_send.at[d], pair_recv.at[d], {"ctx": partner})

    @pl.when(z < CHIPS - 1)
    def _():
        forward(0).start()

    @pl.when(z + NEAR < CHIPS - 1)
    def _():
        direct().start()

    pair(0).start()

    ex_state = remote(
        own_send.at[pl.ds(16 * (1 - core), 16)], part_ref, ex_send.at[0], ex_recv.at[0], {"ctx": partner}
    )
    ex_thr = remote(thr_own, thr_part, ex_send.at[1], ex_recv.at[1], {"ctx": partner})
    ex_state.start()
    ex_thr.start()
    ex_thr.wait_recv()
    ex_state.wait_recv()
    is_first = core == 0
    for t in range(4):
        own = own_ref[pl.ds(16 * core + 4 * t, 4)]
        part = part_ref[4 * t : 4 * t + 4].astype(F32)
        mine, theirs = thr_own[4 * core + t], thr_part[4 * core + t]
        early, late = jnp.where(is_first, own, part), jnp.where(is_first, part, own)
        comb = jnp.where(is_first, theirs, mine)[None] * early + late
        comb_ref[4 * t : 4 * t + 4] = comb.astype(BF16)
        comb_thr[4 * t : 4 * t + 4] = jnp.broadcast_to((mine * theirs)[None], (4, 1, 128))

    def s1(target, source):
        return remote(comb_ref.at[target], in1_ref.at[source], s1_send.at[target], s1_recv.at[source], chip(target))

    def t1(target, source):
        return remote(comb_thr.at[target], thr1_ref.at[source], t1_send.at[target], t1_recv.at[source], chip(target))

    def s2(target, source):
        return remote(pre_ref.at[target], in2_ref.at[source], s2_send.at[target], s2_recv.at[source], chip(target))

    def send1(k, _):
        s1(peer(k), z).start()
        t1(peer(k), z).start()
        return 0

    lax.fori_loop(0, CHIPS - 1, send1, 0)
    in1_ref[z] = comb_ref[z]
    thr1_ref[z] = comb_thr[z]

    for load in loads[5:]:
        load.wait()
    top_ref[...] = jnp.full(top_ref.shape, NEG, F32)
    acc_ref[...] = jnp.zeros(acc_ref.shape, F32)
    heads = q_ref.shape[1] // HD

    def attend(d, causal):
        keys = jnp.concatenate([kv_ref[d, 0, 0], kv_ref[d, 1, 0]], axis=0)
        values = jnp.concatenate([kv_ref[d, 0, 1], kv_ref[d, 1, 1]], axis=0)
        values = jnp.concatenate([values, jnp.ones((2 * TOK, 128), BF16)], axis=1)
        lane = (z - d) * (2 * TOK) + lax.broadcasted_iota(jnp.int32, (TOK, 2 * TOK), 1)
        begin = start_ref[...]
        seen = lane >= jnp.concatenate([begin, begin], axis=1)
        if causal:
            here = qpos_ref[...]
            seen = seen & (lane <= jnp.concatenate([here, here], axis=1))
        for h in range(heads):
            scores = nt_dot(q_ref[:, h * HD : (h + 1) * HD], keys) * SCALE
            scores = jnp.where(seen, scores, NEG)
            before = top_ref[h]
            top = jnp.maximum(before, jnp.max(scores, axis=1, keepdims=True))
            top_ref[h] = top
            fade = jnp.exp2(before - top)
            weights = jnp.exp2(scores - jnp.concatenate([top, top], axis=1)).astype(BF16)
            update = jnp.dot(weights, values, preferred_element_type=F32)
            acc_ref[h] = acc_ref[h] * jnp.concatenate([fade, fade], axis=1) + update

    pair(0).wait_recv()
    attend(0, True)

    def scan():
        def arrive(k, _):
            s1(z, peer(k)).wait_recv()
            t1(z, peer(k)).wait_recv()
            return 0

        lax.fori_loop(0, CHIPS - 1, arrive, 0)
        prefix = jnp.zeros((32, 128), F32)
        for j in range(CHIPS):
            pre_ref[j] = prefix.astype(BF16)
            prefix = thr1_ref[j] * prefix + in1_ref[j].astype(F32)

        def send2(k, _):
            s2(peer(k), z).start()
            return 0

        lax.fori_loop(0, CHIPS - 1, send2, 0)
        in2_ref[z] = pre_ref[z]

    def block(d):
        pair(d).wait_recv()
        attend(d, False)

    def near_arrive(d):
        @pl.when(z >= d)
        def _():
            remote(kv_ref.at[d, core], kv_ref.at[d, core], near_send.at[d], near_recv.at[d], chip(z - d)).wait_recv()

            @pl.when((d < NEAR) & (z < CHIPS - 1))
            def _():
                forward(d).start()

            @pl.when(d > NEAR + 1)
            def _():
                backward(d).start()

            pair(d).start()

    def step(d, _):
        far = FAR + 2 - d

        @pl.when(d <= NEAR)
        def _():
            near_arrive(d)

        @pl.when((far > NEAR) & (far <= FAR))
        def _():
            near_arrive(far)

        @pl.when(d == 4)
        def _():
            scan()

        def late(n, _):
            e = jnp.where(n == 0, d - 1, far + 1)

            @pl.when((e >= 1) & (e <= FAR) & (z >= e) & ((n == 0) | (e > NEAR)))
            def _():
                block(e)

            return 0

        lax.fori_loop(0, 2, late, 0)
        return 0

    lax.fori_loop(1, NEAR + 2, step, 0)

    def arrive2(k, _):
        s2(z, peer(k)).wait_recv()
        return 0

    lax.fori_loop(0, CHIPS - 1, arrive2, 0)
    for t in range(4):
        own = own_ref[pl.ds(16 * core + 4 * t, 4)]
        part = part_ref[4 * t : 4 * t + 4].astype(F32)
        mine, theirs = thr_own[4 * core + t], thr_part[4 * core + t]
        chip_in = in2_ref[4 * t : 4 * t + 4].astype(F32)
        second = jnp.where(is_first, mine, theirs)[None] * chip_in + jnp.where(is_first, own, part)
        state_ref[pl.ds(16 * core + 4 * t, 4)] = jnp.where(is_first, chip_in, second).astype(BF16)
        other_ref[4 * t : 4 * t + 4] = jnp.where(is_first, second, chip_in).astype(BF16)
    half = pl.ds(16 * core, 16)
    theirs_half = pl.ds(16 * (1 - core), 16)
    ex_back = remote(other_ref, state_ref.at[half], ex_send.at[2], ex_recv.at[2], {"ctx": partner})
    ex_back.start()
    for h in range(heads):
        attn_ref[:, h * HD : (h + 1) * HD] = (acc_ref[h, :, 0:HD] / acc_ref[h, :, HD : 2 * HD]).astype(BF16)
    remote(other_ref, state_ref.at[theirs_half], ex_send.at[2], ex_recv.at[2], {"ctx": partner}).wait_recv()

    square = jnp.zeros((TOK, 128), F32)
    er = er_ref[...]
    skip = skip_ref[...]
    for t in range(TILES):
        sl = slice(128 * t, 128 * t + 128)
        rhs = jnp.concatenate([u_ref[:, sl], state_ref[4 * t : 4 * t + 4].reshape(128, 128)], axis=0)
        mixed = jnp.dot(lhs_ref[...], rhs, preferred_element_type=F32) * spread(er, t)
        mixed = mixed + spread(skip, t) * x_ref[:, sl].astype(F32)
        gate = gate_ref[:, sl].astype(F32)
        gated = mixed * (gate / (1.0 + jnp.exp(-gate)))
        gated_ref[:, sl] = gated
        square = square + gated * gated
    norm = lax.rsqrt(jnp.sum(square, axis=1, keepdims=True) * (1.0 / COLS) + 1e-05)
    for t in range(TILES):
        sl = slice(128 * t, 128 * t + 128)
        mamba_ref[:, sl] = (gated_ref[:, sl] * norm * gain_ref[:, sl]).astype(BF16)

    ex_state.wait_send()
    ex_thr.wait_send()
    ex_back.wait_send()

    def sent(k, _):
        s1(peer(k), z).wait_send()
        t1(peer(k), z).wait_send()
        s2(peer(k), z).wait_send()
        return 0

    lax.fori_loop(0, CHIPS - 1, sent, 0)

    @pl.when(z + NEAR < CHIPS - 1)
    def _():
        direct().wait_send()

    def relayed(d, _):
        @pl.when(z >= d)
        def _():
            @pl.when((d < NEAR) & (z < CHIPS - 1))
            def _():
                forward(d).wait_send()

            @pl.when(d > NEAR + 1)
            def _():
                backward(d).wait_send()

            pair(d).wait_send()

        return 0

    lax.fori_loop(0, FAR + 1, relayed, 0)


def per_device(
    mamba_input,
    mamba_gate,
    state_write,
    state_read,
    step_size,
    decay_rate,
    skip_scale,
    norm_gain,
    query_rows,
    key_rows,
    value_rows,
    doc_offsets,
):
    vmem, hbm = pl.BlockSpec(memory_space=pltpu.VMEM), pl.BlockSpec(memory_space=pl.ANY)
    dma = pltpu.SemaphoreType.DMA
    heads = query_rows.shape[1] // HD
    return pl.pallas_call(
        kernel,
        out_shape=(
            jax.ShapeDtypeStruct(mamba_input.shape, BF16),
            jax.ShapeDtypeStruct(query_rows.shape, BF16),
        ),
        in_specs=[pl.BlockSpec(memory_space=pltpu.SMEM)] + [vmem] * 4 + [hbm] * 7,
        out_specs=(vmem, vmem),
        scratch_shapes=[
            pltpu.VMEM((TOK, COLS), BF16),
            pltpu.VMEM((TOK, COLS), BF16),
            pltpu.VMEM((TOK, 128), BF16),
            pltpu.VMEM((TOK, 128), BF16),
            pltpu.VMEM((TOK, heads * HD), BF16),
            pltpu.VMEM((FAR + 1, 2, 2, TOK, HD), BF16),
            pltpu.VMEM((TOK, COLS), BF16),
            pltpu.VMEM((TOK, 256), BF16),
            pltpu.VMEM((TOK, HEADS), F32),
            pltpu.VMEM((32, 32, 128), F32),
            pltpu.VMEM((32, 32, 128), BF16),
            pltpu.VMEM((16, 32, 128), BF16),
            pltpu.VMEM((TILES, 1, 128), F32),
            pltpu.VMEM((TILES, 1, 128), F32),
            pltpu.VMEM((CHIPS, 32, 128), BF16),
            pltpu.VMEM((CHIPS, 1, 128), F32),
            pltpu.VMEM((CHIPS, 32, 128), BF16),
            pltpu.VMEM((CHIPS, 1, 128), F32),
            pltpu.VMEM((CHIPS, 32, 128), BF16),
            pltpu.VMEM((CHIPS, 32, 128), BF16),
            pltpu.VMEM((32, 32, 128), BF16),
            pltpu.VMEM((16, 32, 128), BF16),
            pltpu.VMEM((TOK, 128), jnp.int32),
            pltpu.VMEM((TOK, 128), jnp.int32),
            pltpu.VMEM((heads, TOK, 128), F32),
            pltpu.VMEM((heads, TOK, 256), F32),
            pltpu.VMEM((TOK, COLS), F32),
            dma((7,)),
            dma((FAR + 1,)),
            dma((FAR + 1,)),
            dma((FAR + 1,)),
            dma((FAR + 1,)),
            dma((3,)),
            dma((3,)),
            dma((CHIPS,)),
            dma((CHIPS,)),
            dma((CHIPS,)),
            dma((CHIPS,)),
            dma((CHIPS,)),
            dma((CHIPS,)),
        ],
        compiler_params=pltpu.CompilerParams(collective_id=0, has_side_effects=True, vmem_limit_bytes=48 << 20),
    )(
        doc_offsets,
        step_size,
        decay_rate.reshape(1, -1),
        skip_scale.reshape(1, -1),
        norm_gain.reshape(1, -1),
        mamba_input,
        mamba_gate,
        state_write,
        state_read,
        query_rows,
        key_rows,
        value_rows,
    )


def solution(mesh):
    rows, cols = P(("dp", "ctx"), "tensor"), P("tensor")
    return jax.shard_map(
        per_device,
        mesh=mesh,
        in_specs=(rows,) * 5 + (cols,) * 3 + (rows,) * 3 + (P("dp"),),
        out_specs=(rows, rows),
        check_vma=False,
    )
```

time: 369 us -> 66.5 us (0.18)
  waiting for transfers between devices: 193 us -> 0 us
  local copies, waits for them, and re-layouts: 77.5 us -> 6.53 us
  Pallas kernels: 0 us -> 58.8 us
  blocking collectives: 45.3 us -> 0 us
  other arithmetic: 18.3 us -> 0 us
  matrix products: 16.3 us -> 0 us
  between operations: 14.6 us -> 0.74 us
    all_gather x3 -> x0, waiting for transfers between devices: 192 us -> none  [the longest x1 103 us: entering(): everything = jax.tree.map(lambda part: lax.all_gather(part, axis), value)]
    pallas_call x0 -> x1, Pallas kernels: none -> 58.8 us  [per_device(): pl.pallas_call(kernel, out_shape=(jax.ShapeDtypeStruct(mamba_input.shape,...]
    dynamic_slice x64 -> x0, local copies, waits for them, and re-layouts: 45.3 us -> none  [step(): new = combine(before, jax.tree.map(lambda part: part[k], everything))]
    all_gather x1 -> x0, blocking collectives: 45.3 us -> none  [entering(): everything = jax.tree.map(lambda part: lax.all_gather(part, axis), value)]
    mul x33 -> x0, local copies, waits for them, and re-layouts: 22.2 us -> none  [the longest x32 22.1 us: chain_combine(): later[0][:, None, None] * earlier[1] + later[1]]
    dot_general x6 -> x0, matrix products: 16.3 us -> none  [the longest x1 5.62 us: per_device(): jnp.einsum('gqts,sgd->gqtd', expo.astype(jnp.bfloat16), piece_values.resh...]
    select_n x33 -> x0, other arithmetic: 7.85 us -> none  [the longest x32 7.75 us: step(): return jax.tree.map(lambda a, b: jnp.where(reached, a, b), new, before)]
  transfers between devices with their start and end apart: 3 -> 0, of which waited for: 3 -> 0; matrix products, arithmetic and copies ran while one was open for 7% -> 0% of each run, Pallas kernels for 0% -> 0%
where the time goes in v1:
time: 66.5 us; the launch traced here: 66.1 us
  Pallas kernels  58.8 us (88%)
  local copies, waits for them, and re-layouts  6.53 us (10%)
  between operations  0.74 us (1%)
    pallas_call x1, Pallas kernels, per_device(): pl.pallas_call(kernel, out_shape=(jax.ShapeDtypeStruct(mamba_input.shape,...  58.8 us
    unnamed x25, local copies, waits for them, and re-layouts  6.53 us

profile of v1, /device:TPU:1, one launch (start us, length us, event | category | flops | bytes accessed | tf_op | source)
XLA Modules:
  0.0 66.1 jit_solution(1584115208387361142)
XLA Ops:
  0.6 0.0 copy-start.3
  0.6 0.0 copy-start.4
  0.7 0.0 copy-start.7
  0.7 0.0 copy-start.8
  0.7 0.0 copy-start.9
  0.7 0.0 copy-start.10
  0.7 0.8 %copy.14.step_ref = f32[128,16]{1,0:T(8,128)S(1)} copy(f32[128,16]{0,1:T(8,128)} %param.16) | data formatting | bytes 16384 | tf_op args[4]
  1.5 0.0 copy-done.3
  1.5 0.0 copy-done.4
  1.5 0.0 copy-done.7
  1.5 0.0 copy-done.8
  1.6 0.0 copy-done.9
  1.6 0.0 copy-done.10
  1.6 0.0 copy-start
  1.6 0.9 %copy-done = bf16[128,1024]{1,0:T(8,128)(2,1)S(1)} copy-done((bf16[128,1024]{1,0:T(8,128)(2,1)S(1)}, bf16[128,1024]{1,0:T(8,128)(2,1)}, u32[]{:S(2)}) %copy-start) | copy-done | bytes 262168
  2.5 0.0 copy-start.1
  2.5 0.9 %copy-done.1 = bf16[128,1024]{1,0:T(8,128)(2,1)S(1)} copy-done((bf16[128,1024]{1,0:T(8,128)(2,1)S(1)}, bf16[128,1024]{1,0:T(8,128)(2,1)}, u32[]{:S(2)}) %copy-start.1) | copy-done | bytes 262168
  3.5 0.0 copy-start.2
  3.5 0.9 %copy-done.2 = bf16[128,512]{1,0:T(8,128)(2,1)S(1)} copy-done((bf16[128,512]{1,0:T(8,128)(2,1)S(1)}, bf16[128,512]{1,0:T(8,128)(2,1)}, u32[]{:S(2)}) %copy-start.2) | copy-done | bytes 131096
  4.4 0.8 %copy-done.5 = bf16[128,128]{1,0:T(8,128)(2,1)S(1)} copy-done((bf16[128,128]{1,0:T(8,128)(2,1)S(1)}, bf16[128,128]{1,0:T(8,128)(2,1)}, u32[]{:S(2)}) %copy-start.5) | copy-done | bytes 32792
  5.1 0.8 %copy-done.6 = bf16[128,128]{1,0:T(8,128)(2,1)S(1)} copy-done((bf16[128,128]{1,0:T(8,128)(2,1)S(1)}, bf16[128,128]{1,0:T(8,128)(2,1)}, u32[]{:S(2)}) %copy-start.6) | copy-done | bytes 32792
  5.9 58.8 %shard_map.131 = (bf16[128,1024]{1,0:T(8,128)(2,1)S(1)}, bf16[128,512]{1,0:T(8,128)(2,1)S(1)}) custom-call(s32[33]{0:T(128)S(1)} %copy-done.8, f32[128,16]{1,0:T(8,128)S(1)} %copy.14.step_ref, f32[1,16]{1,0:T(1,128)S(1)} %bitcast.4, f32[1,16]{1,0:T(1,128)S(1)} %bitcast.5, f32[1,1024]{1,0:T(1,128)S(1)} %bitcast.3, bf16[128,1024]{1,0:T(8,128)(2,1)S(1)} %copy-done, ...), custom_call_target="tpu_custom_call" | custom-call | tf_op jit(solution)/shard_map/pallas_call | solution.py:428
  64.7 0.7 %copy.17 = bf16[128,1024]{1,0:T(8,128)(2,1)} copy(bf16[128,1024]{1,0:T(8,128)(2,1)S(1)} %get-tuple-element.4) | data formatting | bytes 524288
  65.4 0.7 copy.18
  (2 shorter events, 0.0 us)
Async XLA Ops:
  0.6 0.9 %copy-start.3 = (bf16[128,128]{1,0:T(8,128)(2,1)S(1)}, bf16[128,128]{1,0:T(8,128)(2,1)}, u32[]{:S(2)}) copy-start(bf16[128,128]{1,0:T(8,128)(2,1)} %write_hbm.1) | copy-start | bytes 98308
  0.6 0.9 %copy-start.4 = (bf16[128,128]{1,0:T(8,128)(2,1)S(1)}, bf16[128,128]{1,0:T(8,128)(2,1)}, u32[]{:S(2)}) copy-start(bf16[128,128]{1,0:T(8,128)(2,1)} %read_hbm.1) | copy-start | bytes 98308
  0.7 0.9 %copy-start.7 = (f32[1024]{0:T(1024)S(1)}, f32[1024]{0:T(1024)}, u32[]{:S(2)}) copy-start(f32[1024]{0:T(1024)} %param.19) | copy-start | bytes 12292
  0.7 0.9 %copy-start.8 = (s32[33]{0:T(128)S(1)}, s32[33]{0:T(128)}, u32[]{:S(2)}) copy-start(s32[33]{0:T(128)} %offs_ref.1) | copy-start | bytes 400
  0.7 0.9 %copy-start.9 = (f32[16]{0:T(128)S(1)}, f32[16]{0:T(128)}, u32[]{:S(2)}) copy-start(f32[16]{0:T(128)} %param.17) | copy-start | bytes 196
  0.7 0.9 %copy-start.10 = (f32[16]{0:T(128)S(1)}, f32[16]{0:T(128)}, u32[]{:S(2)}) copy-start(f32[16]{0:T(128)} %param.18) | copy-start | bytes 196
  1.6 1.0 %copy-start = (bf16[128,1024]{1,0:T(8,128)(2,1)S(1)}, bf16[128,1024]{1,0:T(8,128)(2,1)}, u32[]{:S(2)}) copy-start(bf16[128,1024]{1,0:T(8,128)(2,1)} %x_hbm.1) | copy-start | bytes 786436
  2.5 0.9 %copy-start.1 = (bf16[128,1024]{1,0:T(8,128)(2,1)S(1)}, bf16[128,1024]{1,0:T(8,128)(2,1)}, u32[]{:S(2)}) copy-start(bf16[128,1024]{1,0:T(8,128)(2,1)} %gate_hbm.1) | copy-start | bytes 786436
  3.5 0.9 %copy-start.2 = (bf16[128,512]{1,0:T(8,128)(2,1)S(1)}, bf16[128,512]{1,0:T(8,128)(2,1)}, u32[]{:S(2)}) copy-start(bf16[128,512]{1,0:T(8,128)(2,1)} %q_hbm.1) | copy-start | bytes 393220
  4.4 0.8 %copy-start.5 = (bf16[128,128]{1,0:T(8,128)(2,1)S(1)}, bf16[128,128]{1,0:T(8,128)(2,1)}, u32[]{:S(2)}) copy-start(bf16[128,128]{1,0:T(8,128)(2,1)} %k_hbm.1) | copy-start | bytes 98308
  5.1 0.8 %copy-start.6 = (bf16[128,128]{1,0:T(8,128)(2,1)S(1)}, bf16[128,128]{1,0:T(8,128)(2,1)}, u32[]{:S(2)}) copy-start(bf16[128,128]{1,0:T(8,128)(2,1)} %v_hbm.1) | copy-start | bytes 98308

commit v2 on v1

--- a/solution.py
+++ b/solution.py
@@ -19,7 +19,8 @@
 HEADS = 16
 COLS = HEADS * MP
 TILES = COLS // 128
-NEAR = 7
+HOP = 5
+NEAR = 8
 FAR = 12
 NEG = -1e30
 SCALE = math.log2(math.e) / math.sqrt(HD)
@@ -61,8 +62,10 @@
     q_ref,
     kv_ref,
     u_ref,
-    lhs_ref,
+    carry_ref,
     er_ref,
+    base_ref,
+    silu_ref,
     own_ref,
     own_send,
     part_ref,
@@ -152,10 +155,13 @@
     start_ref[...] = start
     qpos_ref[...] = pos
 
-    lower = (col <= row).astype(F32)
-    running = jnp.dot(lower, -rate_ref[...] * step_ref[...], precision=HIGHEST, preferred_element_type=F32)
-    grow = jnp.exp(-running) * step_ref[...]
-    er_ref[...] = jnp.exp(running)
+    sums = jnp.concatenate([(col <= row).astype(F32), (col == row).astype(F32)], axis=0)
+    sums = lax.dot_general(
+        sums, step_ref[...], (((1,), (1,)), ((), ())), precision=HIGHEST, preferred_element_type=F32
+    )
+    running = -rate_ref[...] * sums[0:TOK]
+    grow = jnp.exp(-running) * sums[TOK : 2 * TOK]
+    er = jnp.exp(running)
     last = jnp.exp(running[TOK - 1 : TOK])
 
     for load in loads[:5]:
@@ -164,8 +170,8 @@
     held_t = held.T.astype(BF16)
     inner = jnp.where((col <= row) & (anchor + col >= start), nt_dot(c_ref[...], b_ref[...]), 0.0)
     entering = jnp.where(start < anchor, c_ref[...].astype(F32), 0.0)
-    lhs_ref[:, 0:128] = inner.astype(BF16)
-    lhs_ref[:, 128:256] = entering.astype(BF16)
+    inner = inner.astype(BF16)
+    carry_ref[...] = entering.astype(BF16)
     for t in range(TILES):
         sl = slice(128 * t, 128 * t + 128)
         u = (x_ref[:, sl].astype(F32) * spread(grow, t)).astype(BF16)
@@ -184,11 +190,16 @@
     def backward(d):
         return remote(kv_ref.at[d, core], kv_ref.at[d - 1, core], near_send.at[d], near_recv.at[d - 1], chip(z - 1))
 
-    def direct():
-        target = jnp.minimum(z + FAR, CHIPS - 1)
+    def direct(target, sem):
         return remote(
-            kv_ref.at[0, core], kv_ref.at[target - z, core], near_send.at[NEAR], near_recv.at[target - z], chip(target)
+            kv_ref.at[0, core], kv_ref.at[target - z, core], near_send.at[sem], near_recv.at[target - z], chip(target)
         )
+
+    def leap():
+        return direct(z + HOP, FAR + 1)
+
+    def round_back():
+        return direct(jnp.minimum(z + FAR, CHIPS - 1), FAR + 2)
 
     def pair(d):
         return remote(kv_ref.at[d, core], kv_ref.at[d, core], pair_send.at[d], pair_recv.at[d], {"ctx": partner})
@@ -196,10 +207,6 @@
     @pl.when(z < CHIPS - 1)
     def _():
         forward(0).start()
-
-    @pl.when(z + NEAR < CHIPS - 1)
-    def _():
-        direct().start()
 
     pair(0).start()
 
@@ -236,6 +243,15 @@
         return 0
 
     lax.fori_loop(0, CHIPS - 1, send1, 0)
+
+    @pl.when(z + HOP < CHIPS)
+    def _():
+        leap().start()
+
+    @pl.when(z + NEAR < CHIPS - 1)
+    def _():
+        round_back().start()
+
     in1_ref[z] = comb_ref[z]
     thr1_ref[z] = comb_thr[z]
 
@@ -269,6 +285,17 @@
     pair(0).wait_recv()
     attend(0, True)
 
+    skip = skip_ref[...]
+    for t in range(TILES):
+        sl = slice(128 * t, 128 * t + 128)
+        decay = spread(er, t)
+        er_ref[t] = decay
+        base_ref[t] = jnp.dot(inner, u_ref[:, sl], preferred_element_type=F32) * decay + spread(skip, t) * x_ref[
+            :, sl
+        ].astype(F32)
+        gate = gate_ref[:, sl].astype(F32)
+        silu_ref[t] = gate / (1.0 + jnp.exp(-gate))
+
     def scan():
         def arrive(k, _):
             s1(z, peer(k)).wait_recv()
@@ -297,7 +324,7 @@
         def _():
             remote(kv_ref.at[d, core], kv_ref.at[d, core], near_send.at[d], near_recv.at[d], chip(z - d)).wait_recv()
 
-            @pl.when((d < NEAR) & (z < CHIPS - 1))
+            @pl.when((d < NEAR) & (d != HOP - 1) & (z < CHIPS - 1))
             def _():
                 forward(d).start()
 
@@ -307,34 +334,40 @@
 
             pair(d).start()
 
-    def step(d, _):
-        far = FAR + 2 - d
-
-        @pl.when(d <= NEAR)
-        def _():
-            near_arrive(d)
-
-        @pl.when((far > NEAR) & (far <= FAR))
-        def _():
-            near_arrive(far)
-
-        @pl.when(d == 4)
+    def step(n, _):
+        @pl.when(n < HOP)
+        def _():
+            near_arrive(n)
+
+        @pl.when(n == 1)
         def _():
             scan()
 
-        def late(n, _):
-            e = jnp.where(n == 0, d - 1, far + 1)
-
-            @pl.when((e >= 1) & (e <= FAR) & (z >= e) & ((n == 0) | (e > NEAR)))
+        @pl.when(n + HOP - 1 <= NEAR)
+        def _():
+            near_arrive(n + HOP - 1)
+
+        @pl.when(FAR + 1 - n > NEAR)
+        def _():
+            near_arrive(FAR + 1 - n)
+
+        def late(i, _):
+            e = jnp.where(i == 0, n - 1, jnp.where(i == 1, n + HOP - 2, FAR + 2 - n))
+            inside = jnp.where(i == 0, e < HOP, jnp.where(i == 1, e <= NEAR, e > NEAR))
+
+            @pl.when(inside & (z >= e))
             def _():
                 block(e)
 
             return 0
 
-        lax.fori_loop(0, 2, late, 0)
+        @pl.when(n > 1)
+        def _():
+            lax.fori_loop(0, 3, late, 0)
+
         return 0
 
-    lax.fori_loop(1, NEAR + 2, step, 0)
+    lax.fori_loop(1, FAR - NEAR + 2, step, 0)
 
     def arrive2(k, _):
         s2(z, peer(k)).wait_recv()
@@ -355,24 +388,24 @@
     ex_back.start()
     for h in range(heads):
         attn_ref[:, h * HD : (h + 1) * HD] = (acc_ref[h, :, 0:HD] / acc_ref[h, :, HD : 2 * HD]).astype(BF16)
+
+    def finish(side, square):
+        for t in range(4):
+            tile = 4 * side + t
+            state = state_ref[pl.ds(4 * tile, 4)].reshape(128, 128)
+            mixed = base_ref[tile] + er_ref[tile] * jnp.dot(carry_ref[...], state, preferred_element_type=F32)
+            gated = mixed * silu_ref[tile]
+            gated_ref[tile] = gated
+            square = square + gated * gated
+        return square
+
+    square = finish(core, jnp.zeros((TOK, 128), F32))
     remote(other_ref, state_ref.at[theirs_half], ex_send.at[2], ex_recv.at[2], {"ctx": partner}).wait_recv()
-
-    square = jnp.zeros((TOK, 128), F32)
-    er = er_ref[...]
-    skip = skip_ref[...]
-    for t in range(TILES):
-        sl = slice(128 * t, 128 * t + 128)
-        rhs = jnp.concatenate([u_ref[:, sl], state_ref[4 * t : 4 * t + 4].reshape(128, 128)], axis=0)
-        mixed = jnp.dot(lhs_ref[...], rhs, preferred_element_type=F32) * spread(er, t)
-        mixed = mixed + spread(skip, t) * x_ref[:, sl].astype(F32)
-        gate = gate_ref[:, sl].astype(F32)
-        gated = mixed * (gate / (1.0 + jnp.exp(-gate)))
-        gated_ref[:, sl] = gated
-        square = square + gated * gated
+    square = finish(1 - core, square)
     norm = lax.rsqrt(jnp.sum(square, axis=1, keepdims=True) * (1.0 / COLS) + 1e-05)
     for t in range(TILES):
         sl = slice(128 * t, 128 * t + 128)
-        mamba_ref[:, sl] = (gated_ref[:, sl] * norm * gain_ref[:, sl]).astype(BF16)
+        mamba_ref[:, sl] = (gated_ref[t] * norm * gain_ref[:, sl]).astype(BF16)
 
     ex_state.wait_send()
     ex_thr.wait_send()
@@ -386,14 +419,18 @@
 
     lax.fori_loop(0, CHIPS - 1, sent, 0)
 
+    @pl.when(z + HOP < CHIPS)
+    def _():
+        leap().wait_send()
+
     @pl.when(z + NEAR < CHIPS - 1)
     def _():
-        direct().wait_send()
+        round_back().wait_send()
 
     def relayed(d, _):
         @pl.when(z >= d)
         def _():
-            @pl.when((d < NEAR) & (z < CHIPS - 1))
+            @pl.when((d < NEAR) & (d != HOP - 1) & (z < CHIPS - 1))
             def _():
                 forward(d).wait_send()
 
@@ -441,8 +478,10 @@
             pltpu.VMEM((TOK, heads * HD), BF16),
             pltpu.VMEM((FAR + 1, 2, 2, TOK, HD), BF16),
             pltpu.VMEM((TOK, COLS), BF16),
-            pltpu.VMEM((TOK, 256), BF16),
-            pltpu.VMEM((TOK, HEADS), F32),
+            pltpu.VMEM((TOK, 128), BF16),
+            pltpu.VMEM((TILES, TOK, 128), F32),
+            pltpu.VMEM((TILES, TOK, 128), F32),
+            pltpu.VMEM((TILES, TOK, 128), F32),
             pltpu.VMEM((32, 32, 128), F32),
             pltpu.VMEM((32, 32, 128), BF16),
             pltpu.VMEM((16, 32, 128), BF16),
@@ -460,11 +499,11 @@
             pltpu.VMEM((TOK, 128), jnp.int32),
             pltpu.VMEM((heads, TOK, 128), F32),
             pltpu.VMEM((heads, TOK, 256), F32),
-            pltpu.VMEM((TOK, COLS), F32),
+            pltpu.VMEM((TILES, TOK, 128), F32),
             dma((7,)),
             dma((FAR + 1,)),
             dma((FAR + 1,)),
-            dma((FAR + 1,)),
+            dma((FAR + 3,)),
             dma((FAR + 1,)),
             dma((3,)),
             dma((3,)),
@@ -475,10 +514,10 @@
             dma((CHIPS,)),
             dma((CHIPS,)),
         ],
-        compiler_params=pltpu.CompilerParams(collective_id=0, has_side_effects=True, vmem_limit_bytes=48 << 20),
+        compiler_params=pltpu.CompilerParams(collective_id=0, has_side_effects=True),
     )(
         doc_offsets,
-        step_size,
+        step_size.T,
         decay_rate.reshape(1, -1),
         skip_scale.reshape(1, -1),
         norm_gain.reshape(1, -1),

time: 66.5 us -> 52.1 us (0.78)
  the two profiles are of different devices: /device:TPU:1 before, /device:TPU:693 now
where the time goes in v2:
time: 52.1 us; the launch traced here: 51.8 us
  Pallas kernels  48.8 us (94%)
  local copies, waits for them, and re-layouts  2.36 us (5%)
  between operations  0.65 us (1%)
    pallas_call x1, Pallas kernels, per_device(): pl.pallas_call(kernel, out_shape=(jax.ShapeDtypeStruct(mamba_input.shape,...  48.8 us
    unnamed x4, local copies, waits for them, and re-layouts  2.36 us

profile of v2, /device:TPU:693, one launch (start us, length us, event | category | flops | bytes accessed | tf_op | source)
XLA Modules:
  0.0 51.8 jit_solution(4071019228733143559)
XLA Ops:
  0.6 48.8 %shard_map.131 = (bf16[128,1024]{1,0:T(8,128)(2,1)}, bf16[128,512]{1,0:T(8,128)(2,1)}) custom-call(s32[33]{0:T(128)} %offs_ref.1, f32[16,128]{1,0:T(8,128)} %bitcast.4, f32[1,16]{1,0:T(1,128)} %bitcast.6, f32[1,16]{1,0:T(1,128)} %bitcast.7, f32[1,1024]{1,0:T(1,128)} %bitcast.5, bf16[128,1024]{1,0:T(8,128)(2,1)} %x_hbm.1, bf16[128,1024]{1,0:T(8,128)(2,1)} %gate_hbm.1, ...), custom_call_target="tpu_custom_call" | custom-call | tf_op jit(solution)/shard_map/pallas_call | solution.py:465
  49.5 0.0 copy-start
  49.5 1.7 %copy.16 = bf16[128,1024]{1,0:T(8,128)(2,1)} copy(bf16[128,1024]{1,0:T(8,128)(2,1)} %get-tuple-element.4) | data formatting | bytes 524288
  51.2 0.0 copy-done
  51.2 0.7 %copy.17 = bf16[128,512]{1,0:T(8,128)(2,1)} copy(bf16[128,512]{1,0:T(8,128)(2,1)S(1)} %copy-done) | data formatting | bytes 262144
Async XLA Ops:
  49.5 1.7 %copy-start = (bf16[128,512]{1,0:T(8,128)(2,1)S(1)}, bf16[128,512]{1,0:T(8,128)(2,1)}, u32[]{:S(2)}) copy-start(bf16[128,512]{1,0:T(8,128)(2,1)} %get-tuple-element.5) | copy-start | bytes 393220

commit v3 on v2

--- a/solution.py
+++ b/solution.py
@@ -20,8 +20,9 @@
 COLS = HEADS * MP
 TILES = COLS // 128
 HOP = 5
-NEAR = 8
+NEAR = 9
 FAR = 12
+STEPS = max(HOP - 1, NEAR - HOP + 1, FAR - NEAR) + 1
 NEG = -1e30
 SCALE = math.log2(math.e) / math.sqrt(HD)
 
@@ -129,11 +130,11 @@
         pltpu.make_async_copy(src, dst, load_sem.at[n])
         for n, (src, dst) in enumerate(
             (
+                (write_hbm, b_ref),
+                (x_hbm, x_ref),
                 (k_hbm, kv_ref.at[0, core, 0]),
                 (v_hbm, kv_ref.at[0, core, 1]),
-                (write_hbm, b_ref),
                 (read_hbm, c_ref),
-                (x_hbm, x_ref),
                 (q_hbm, q_ref),
                 (gate_hbm, gate_ref),
             )
@@ -164,14 +165,10 @@
     er = jnp.exp(running)
     last = jnp.exp(running[TOK - 1 : TOK])
 
-    for load in loads[:5]:
+    for load in loads[:2]:
         load.wait()
     held = jnp.where(pos >= final, b_ref[...].astype(F32), 0.0)
     held_t = held.T.astype(BF16)
-    inner = jnp.where((col <= row) & (anchor + col >= start), nt_dot(c_ref[...], b_ref[...]), 0.0)
-    entering = jnp.where(start < anchor, c_ref[...].astype(F32), 0.0)
-    inner = inner.astype(BF16)
-    carry_ref[...] = entering.astype(BF16)
     for t in range(TILES):
         sl = slice(128 * t, 128 * t + 128)
         u = (x_ref[:, sl].astype(F32) * spread(grow, t)).astype(BF16)
@@ -182,31 +179,35 @@
         own_send[4 * t : 4 * t + 4] = tile.astype(BF16).reshape(4, 32, 128)
         thr_own[t] = jnp.where(final < anchor, decay, 0.0)
 
+    for load in loads[2:4]:
+        load.wait()
     pl.semaphore_wait(barrier, CHIPS)
 
-    def forward(d):
-        return remote(kv_ref.at[d, core], kv_ref.at[d + 1, core], near_send.at[d], near_recv.at[d + 1], chip(z + 1))
-
-    def backward(d):
-        return remote(kv_ref.at[d, core], kv_ref.at[d - 1, core], near_send.at[d], near_recv.at[d - 1], chip(z - 1))
-
-    def direct(target, sem):
+    def hop(d, e, part, sem, device):
         return remote(
-            kv_ref.at[0, core], kv_ref.at[target - z, core], near_send.at[sem], near_recv.at[target - z], chip(target)
+            kv_ref.at[d, core, part], kv_ref.at[e, core, part], near_send.at[sem, part], near_recv.at[e, part], device
         )
 
-    def leap():
-        return direct(z + HOP, FAR + 1)
-
-    def round_back():
-        return direct(jnp.minimum(z + FAR, CHIPS - 1), FAR + 2)
+    def forward(d, part):
+        return hop(d, d + 1, part, d, chip(z + 1))
+
+    def backward(d, part):
+        return hop(d, d - 1, part, d, chip(z - 1))
+
+    def leap(part):
+        return hop(0, HOP, part, FAR + 1, chip(z + HOP))
+
+    def round_back(part):
+        target = jnp.minimum(z + FAR, CHIPS - 1)
+        return hop(0, target - z, part, FAR + 2, chip(target))
 
     def pair(d):
         return remote(kv_ref.at[d, core], kv_ref.at[d, core], pair_send.at[d], pair_recv.at[d], {"ctx": partner})
 
     @pl.when(z < CHIPS - 1)
     def _():
-        forward(0).start()
+        forward(0, 0).start()
+        forward(0, 1).start()
 
     pair(0).start()
 
@@ -246,16 +247,18 @@
 
     @pl.when(z + HOP < CHIPS)
     def _():
-        leap().start()
+        leap(0).start()
+        leap(1).start()
 
     @pl.when(z + NEAR < CHIPS - 1)
     def _():
-        round_back().start()
+        round_back(0).start()
+        round_back(1).start()
 
     in1_ref[z] = comb_ref[z]
     thr1_ref[z] = comb_thr[z]
 
-    for load in loads[5:]:
+    for load in loads[4:]:
         load.wait()
     top_ref[...] = jnp.full(top_ref.shape, NEG, F32)
     acc_ref[...] = jnp.zeros(acc_ref.shape, F32)
@@ -285,6 +288,8 @@
     pair(0).wait_recv()
     attend(0, True)
 
+    inner = jnp.where((col <= row) & (anchor + col >= start), nt_dot(c_ref[...], b_ref[...]), 0.0).astype(BF16)
+    carry_ref[...] = jnp.where(start < anchor, c_ref[...].astype(F32), 0.0).astype(BF16)
     skip = skip_ref[...]
     for t in range(TILES):
         sl = slice(128 * t, 128 * t + 128)
@@ -322,15 +327,16 @@
     def near_arrive(d):
         @pl.when(z >= d)
         def _():
-            remote(kv_ref.at[d, core], kv_ref.at[d, core], near_send.at[d], near_recv.at[d], chip(z - d)).wait_recv()
-
-            @pl.when((d < NEAR) & (d != HOP - 1) & (z < CHIPS - 1))
-            def _():
-                forward(d).start()
-
-            @pl.when(d > NEAR + 1)
-            def _():
-                backward(d).start()
+            for part in range(2):
+                hop(d, d, part, d, chip(z - d)).wait_recv()
+
+                @pl.when((d < NEAR) & (d != HOP - 1) & (z < CHIPS - 1))
+                def _(part=part):
+                    forward(d, part).start()
+
+                @pl.when(d > NEAR + 1)
+                def _(part=part):
+                    backward(d, part).start()
 
             pair(d).start()
 
@@ -367,7 +373,7 @@
 
         return 0
 
-    lax.fori_loop(1, FAR - NEAR + 2, step, 0)
+    lax.fori_loop(1, STEPS + 1, step, 0)
 
     def arrive2(k, _):
         s2(z, peer(k)).wait_recv()
@@ -421,22 +427,26 @@
 
     @pl.when(z + HOP < CHIPS)
     def _():
-        leap().wait_send()
+        leap(0).wait_send()
+        leap(1).wait_send()
 
     @pl.when(z + NEAR < CHIPS - 1)
     def _():
-        round_back().wait_send()
+        round_back(0).wait_send()
+        round_back(1).wait_send()
 
     def relayed(d, _):
         @pl.when(z >= d)
         def _():
             @pl.when((d < NEAR) & (d != HOP - 1) & (z < CHIPS - 1))
             def _():
-                forward(d).wait_send()
+                forward(d, 0).wait_send()
+                forward(d, 1).wait_send()
 
             @pl.when(d > NEAR + 1)
             def _():
-                backward(d).wait_send()
+                backward(d, 0).wait_send()
+                backward(d, 1).wait_send()
 
             pair(d).wait_send()
 
@@ -501,9 +511,9 @@
             pltpu.VMEM((heads, TOK, 256), F32),
             pltpu.VMEM((TILES, TOK, 128), F32),
             dma((7,)),
+            dma((FAR + 1, 2)),
             dma((FAR + 1,)),
-            dma((FAR + 1,)),
-            dma((FAR + 3,)),
+            dma((FAR + 3, 2)),
             dma((FAR + 1,)),
             dma((3,)),
             dma((3,)),

time: 52.1 us -> 52.7 us (1.012)
  the two profiles are of different devices: /device:TPU:693 before, /device:TPU:581 now
where the time goes in v3:
time: 52.7 us; the launch traced here: 52.5 us
  Pallas kernels  49.5 us (94%)
  local copies, waits for them, and re-layouts  2.36 us (4%)
  between operations  0.65 us (1%)
    pallas_call x1, Pallas kernels, per_device(): pl.pallas_call(kernel, out_shape=(jax.ShapeDtypeStruct(mamba_input.shape,...  49.5 us
    unnamed x4, local copies, waits for them, and re-layouts  2.36 us

profile of v3, /device:TPU:581, one launch (start us, length us, event | category | flops | bytes accessed | tf_op | source)
XLA Modules:
  0.0 52.5 jit_solution(17842397607307125644)
XLA Ops:
  0.6 49.5 %shard_map.131 = (bf16[128,1024]{1,0:T(8,128)(2,1)}, bf16[128,512]{1,0:T(8,128)(2,1)}) custom-call(s32[33]{0:T(128)} %offs_ref.1, f32[16,128]{1,0:T(8,128)} %bitcast.4, f32[1,16]{1,0:T(1,128)} %bitcast.6, f32[1,16]{1,0:T(1,128)} %bitcast.7, f32[1,1024]{1,0:T(1,128)} %bitcast.5, bf16[128,1024]{1,0:T(8,128)(2,1)} %x_hbm.1, bf16[128,1024]{1,0:T(8,128)(2,1)} %gate_hbm.1, ...), custom_call_target="tpu_custom_call" | custom-call | tf_op jit(solution)/shard_map/pallas_call | solution.py:475
  50.1 0.0 copy-start
  50.1 1.7 %copy.16 = bf16[128,1024]{1,0:T(8,128)(2,1)} copy(bf16[128,1024]{1,0:T(8,128)(2,1)} %get-tuple-element.4) | data formatting | bytes 524288
  51.8 0.0 copy-done
  51.9 0.7 %copy.17 = bf16[128,512]{1,0:T(8,128)(2,1)} copy(bf16[128,512]{1,0:T(8,128)(2,1)S(1)} %copy-done) | data formatting | bytes 262144
Async XLA Ops:
  50.1 1.7 %copy-start = (bf16[128,512]{1,0:T(8,128)(2,1)S(1)}, bf16[128,512]{1,0:T(8,128)(2,1)}, u32[]{:S(2)}) copy-start(bf16[128,512]{1,0:T(8,128)(2,1)} %get-tuple-element.5) | copy-start | bytes 393220

commit v4 on v3

--- a/solution.py
+++ b/solution.py
@@ -20,7 +20,7 @@
 COLS = HEADS * MP
 TILES = COLS // 128
 HOP = 5
-NEAR = 9
+NEAR = 8
 FAR = 12
 STEPS = max(HOP - 1, NEAR - HOP + 1, FAR - NEAR) + 1
 NEG = -1e30
@@ -475,8 +475,8 @@
     return pl.pallas_call(
         kernel,
         out_shape=(
-            jax.ShapeDtypeStruct(mamba_input.shape, BF16),
-            jax.ShapeDtypeStruct(query_rows.shape, BF16),
+            pltpu.VMEM(mamba_input.shape, BF16),
+            pltpu.VMEM(query_rows.shape, BF16),
         ),
         in_specs=[pl.BlockSpec(memory_space=pltpu.SMEM)] + [vmem] * 4 + [hbm] * 7,
         out_specs=(vmem, vmem),

time: 52.7 us -> 49.6 us (0.941)
  the two profiles are of different devices: /device:TPU:581 before, /device:TPU:1 now
where the time goes in v4:
time: 49.6 us; the launch traced here: 49.4 us
  Pallas kernels  47.4 us (96%)
  local copies, waits for them, and re-layouts  1.36 us (3%)
  between operations  0.64 us (1%)
    pallas_call x1, Pallas kernels, per_device(): pl.pallas_call(kernel, out_shape=(pltpu.VMEM(mamba_input.shape, BF16), pl...  47.4 us
    unnamed x2, local copies, waits for them, and re-layouts  1.36 us

profile of v4, /device:TPU:1, one launch (start us, length us, event | category | flops | bytes accessed | tf_op | source)
XLA Modules:
  0.0 49.4 jit_solution(890302480305277557)
XLA Ops:
  0.6 47.4 %shard_map.131 = (bf16[128,1024]{1,0:T(8,128)(2,1)S(1)}, bf16[128,512]{1,0:T(8,128)(2,1)S(1)}) custom-call(s32[33]{0:T(128)} %offs_ref.1, f32[16,128]{1,0:T(8,128)} %bitcast.4, f32[1,16]{1,0:T(1,128)} %bitcast.6, f32[1,16]{1,0:T(1,128)} %bitcast.7, f32[1,1024]{1,0:T(1,128)} %bitcast.5, bf16[128,1024]{1,0:T(8,128)(2,1)} %x_hbm.1, bf16[128,1024]{1,0:T(8,128)(2,1)} %gate_hbm.1, ...), custom_call_target="tpu_custom_call" | custom-call | tf_op jit(solution)/shard_map/pallas_call | solution.py:475
  48.1 0.7 %copy.16 = bf16[128,1024]{1,0:T(8,128)(2,1)} copy(bf16[128,1024]{1,0:T(8,128)(2,1)S(1)} %get-tuple-element.2) | data formatting | bytes 524288
  48.8 0.7 %copy.17 = bf16[128,512]{1,0:T(8,128)(2,1)} copy(bf16[128,512]{1,0:T(8,128)(2,1)S(1)} %get-tuple-element.3) | data formatting | bytes 262144

commit v5 on v4

--- a/solution.py
+++ b/solution.py
@@ -245,15 +245,15 @@
 
     lax.fori_loop(0, CHIPS - 1, send1, 0)
 
+    @pl.when(z + NEAR < CHIPS - 1)
+    def _():
+        round_back(0).start()
+        round_back(1).start()
+
     @pl.when(z + HOP < CHIPS)
     def _():
         leap(0).start()
         leap(1).start()
-
-    @pl.when(z + NEAR < CHIPS - 1)
-    def _():
-        round_back(0).start()
-        round_back(1).start()
 
     in1_ref[z] = comb_ref[z]
     thr1_ref[z] = comb_thr[z]

time: 49.6 us -> 49.6 us (level)
  no operation moved by 1% of the time
where the time goes in v5:
time: 49.6 us; the launch traced here: 49.4 us
  Pallas kernels  47.4 us (96%)
  local copies, waits for them, and re-layouts  1.36 us (3%)
  between operations  0.64 us (1%)
    pallas_call x1, Pallas kernels, per_device(): pl.pallas_call(kernel, out_shape=(pltpu.VMEM(mamba_input.shape, BF16), pl...  47.4 us
    unnamed x2, local copies, waits for them, and re-layouts  1.36 us

profile of v5, /device:TPU:1, one launch (start us, length us, event | category | flops | bytes accessed | tf_op | source)
XLA Modules:
  0.0 49.4 jit_solution(16101256289084797688)
XLA Ops:
  0.6 47.4 %shard_map.131 = (bf16[128,1024]{1,0:T(8,128)(2,1)S(1)}, bf16[128,512]{1,0:T(8,128)(2,1)S(1)}) custom-call(s32[33]{0:T(128)} %offs_ref.1, f32[16,128]{1,0:T(8,128)} %bitcast.4, f32[1,16]{1,0:T(1,128)} %bitcast.6, f32[1,16]{1,0:T(1,128)} %bitcast.7, f32[1,1024]{1,0:T(1,128)} %bitcast.5, bf16[128,1024]{1,0:T(8,128)(2,1)} %x_hbm.1, bf16[128,1024]{1,0:T(8,128)(2,1)} %gate_hbm.1, ...), custom_call_target="tpu_custom_call" | custom-call | tf_op jit(solution)/shard_map/pallas_call | solution.py:475
  48.1 0.7 %copy.16 = bf16[128,1024]{1,0:T(8,128)(2,1)} copy(bf16[128,1024]{1,0:T(8,128)(2,1)S(1)} %get-tuple-element.2) | data formatting | bytes 524288
  48.8 0.7 %copy.17 = bf16[128,512]{1,0:T(8,128)(2,1)} copy(bf16[128,512]{1,0:T(8,128)(2,1)S(1)} %get-tuple-element.3) | data formatting | bytes 262144
